TPU v7x, 32 devices: a whole 2x2x4 slice. The times are simulated.
32 devices in a mesh: clips: 2 (over y), sa: 4 (over z), wa: 2 (over x), hp: 2 (over core).
Axes of the slice: x: 2, y: 2, z: 4, core: 2. Of those that a mesh axis runs over, the one named last changes fastest.
Arguments:
- queries: bfloat16 [16, 8, 16, 3072], P(('clips', 'sa'), None, 'wa', 'hp'), parts along dimension 0, may hold values from -6 to 6
- keys: bfloat16 [16, 8, 16, 3072], P(('clips', 'sa'), None, 'wa', 'hp'), parts along dimension 0, may hold values from -6 to 6
- values: bfloat16 [16, 8, 16, 3072], P(('clips', 'sa'), None, 'wa', 'hp'), parts along dimension 0, may hold values from -6 to 6
- text_keys: bfloat16 [512, 3072], P(('clips', 'sa'), 'hp'), parts along dimension 0, may hold values from -6 to 6
- text_values: bfloat16 [512, 3072], P(('clips', 'sa'), 'hp'), parts along dimension 0, may hold values from -6 to 6
- out_grad: bfloat16 [16, 8, 16, 3072], P(('clips', 'sa'), None, 'wa', 'hp'), parts along dimension 0, may hold values from -6 to 6
- window_ext: int32 [24, 3], P('hp'), may hold values from 0 to 1, as said below
Outputs:
- attended: bfloat16 [16, 8, 16, 3072], P(('clips', 'sa'), None, 'wa', 'hp'), parts along dimension 0
- query_grad: bfloat16 [16, 8, 16, 3072], P(('clips', 'sa'), None, 'wa', 'hp'), parts along dimension 0
- key_grad: bfloat16 [16, 8, 16, 3072], P(('clips', 'sa'), None, 'wa', 'hp'), parts along dimension 0
- value_grad: bfloat16 [16, 8, 16, 3072], P(('clips', 'sa'), None, 'wa', 'hp'), parts along dimension 0
- text_key_grad: float32 [512, 3072], P(('clips', 'sa'), 'hp'), parts along dimension 0
- text_value_grad: float32 [512, 3072], P(('clips', 'sa'), 'hp'), parts along dimension 0
There are 2 independent parts, one for each index of `clips`. A program takes and returns all parts, laid end to end along the dimension named above; an argument that names none is the same for every part. Nothing has to cross between parts.
Inputs may be any that keep to these rules, and one draw needn't show every extreme that they name: `window_ext`: columns 0, 1 and 2 are at most 1, 1 and 1; each of these bounds is reached by some head.
All inputs are finite; a program needn't handle non-finite values.
Results may differ from a plain program's by a relative error of at most 0.012.
The roundings to bfloat16 on the way count: a program that leaves them out, or rounds other values in their place, can miss the bound.
Values may be sent and summed in bfloat16 or wider, within the bound.
A program may use at most 128 MiB of HBM per device.

v0:
```python
import jax
import jax.numpy as jnp
from jax import lax
from jax.sharding import PartitionSpec as P

HEAD_DIM = 128
TILE_T = 2
TILE_H = 8
TILE_W = 8
EXT_T = 1
EXT_W = 1


def with_halo(array, sides, width):
    for axis, dim in sides:
        size, length = (lax.axis_size(axis), array.shape[dim])
        up = [(i, (i + 1) % size) for i in range(size - 1)]
        down = [(j, i) for i, j in up]
        last = lax.slice_in_dim(array, length - width, length, axis=dim)
        first = lax.slice_in_dim(array, 0, width, axis=dim)
        before = lax.ppermute(last, axis, up)
        after = lax.ppermute(first, axis, down)
        array = jnp.concatenate([before, array, after], axis=dim)
    return array


def tile_coords(time_start, frame_count, row_count, col_start, col_count, total_frames, total_cols):
    times = time_start + jnp.arange(frame_count, dtype=jnp.int32)
    heights = jnp.arange(row_count, dtype=jnp.int32)
    columns = col_start + jnp.arange(col_count, dtype=jnp.int32)
    grid_shape = (frame_count, row_count, col_count)
    time_grid = jnp.broadcast_to(times[:, None, None], grid_shape).reshape(-1)
    height_grid = jnp.broadcast_to(heights[None, :, None], grid_shape).reshape(-1)
    col_grid = jnp.broadcast_to(columns[None, None, :], grid_shape).reshape(-1)
    inside = (
        (time_grid >= 0) & (time_grid < total_frames) & (col_grid >= 0) & (col_grid < total_cols)
    )
    return (time_grid // TILE_T, height_grid // TILE_H, col_grid // TILE_W, inside)


def pair_mask(first, second, window):
    allowed = first[3][:, None] & second[3][None, :]
    for axis_number in range(3):
        apart = jnp.abs(first[axis_number][:, None] - second[axis_number][None, :])
        allowed = allowed & (apart <= window[axis_number])
    return allowed


def forward_head(query_head, key_head, value_head, text_key, text_value, allowed):
    score_scale = HEAD_DIM ** (-0.5)
    video_scores = jnp.dot(query_head, key_head.T, preferred_element_type=jnp.float32) * score_scale
    video_scores = jnp.where(allowed, video_scores, -1e30)
    text_scores = jnp.dot(query_head, text_key.T, preferred_element_type=jnp.float32) * score_scale
    row_max = jnp.maximum(jnp.max(video_scores, axis=1), jnp.max(text_scores, axis=1))
    denom_sum = jnp.sum(jnp.exp(video_scores - row_max[:, None]), axis=1) + jnp.sum(
        jnp.exp(text_scores - row_max[:, None]), axis=1
    )
    log_total = row_max + jnp.log(denom_sum)
    video_weights = jnp.exp(video_scores - log_total[:, None]).astype(jnp.bfloat16)
    text_weights = jnp.exp(text_scores - log_total[:, None]).astype(jnp.bfloat16)
    attended_head = jnp.dot(video_weights, value_head, preferred_element_type=jnp.float32)
    attended_head = attended_head + jnp.dot(
        text_weights, text_value, preferred_element_type=jnp.float32
    )
    return (attended_head.astype(jnp.bfloat16), log_total)


def grads_head(
    query_head, grad_head, log_total, row_delta, key_head, value_head, text_key, text_value, allowed
):
    score_scale = HEAD_DIM ** (-0.5)
    video_scores = jnp.dot(query_head, key_head.T, preferred_element_type=jnp.float32) * score_scale
    video_scores = jnp.where(allowed, video_scores, -1e30)
    text_scores = jnp.dot(query_head, text_key.T, preferred_element_type=jnp.float32) * score_scale
    video_probs = jnp.exp(video_scores - log_total[:, None])
    text_probs = jnp.exp(text_scores - log_total[:, None])
    video_dprobs = jnp.dot(grad_head, value_head.T, preferred_element_type=jnp.float32)
    text_dprobs = jnp.dot(grad_head, text_value.T, preferred_element_type=jnp.float32)
    video_dscores = (video_probs * (video_dprobs - row_delta[:, None]) * score_scale).astype(
        jnp.bfloat16
    )
    text_dscores = (text_probs * (text_dprobs - row_delta[:, None]) * score_scale).astype(
        jnp.bfloat16
    )
    query_term = jnp.dot(video_dscores, key_head, preferred_element_type=jnp.float32)
    query_term = query_term + jnp.dot(text_dscores, text_key, preferred_element_type=jnp.float32)
    key_term = jnp.dot(video_dscores.T, query_head, preferred_element_type=jnp.float32)
    value_term = jnp.dot(
        video_probs.astype(jnp.bfloat16).T, grad_head, preferred_element_type=jnp.float32
    )
    text_key_term = jnp.dot(text_dscores.T, query_head, preferred_element_type=jnp.float32)
    text_value_term = jnp.dot(
        text_probs.astype(jnp.bfloat16).T, grad_head, preferred_element_type=jnp.float32
    )
    return (query_term, key_term, value_term, text_key_term, text_value_term)


def shards(queries, keys, values, text_keys, text_values, out_grad, window_ext):
    rim_time = EXT_T * TILE_T
    rim_cols = EXT_W * TILE_W
    frames, row_count, col_count, channels = queries.shape
    heads_dev = channels // HEAD_DIM
    total_frames = frames * lax.axis_size("sa")
    total_cols = col_count * lax.axis_size("wa")
    time_start = lax.axis_index("sa") * frames
    col_start = lax.axis_index("wa") * col_count
    own_cells = tile_coords(
        time_start, frames, row_count, col_start, col_count, total_frames, total_cols
    )
    near_cells = tile_coords(
        time_start - rim_time,
        frames + 2 * rim_time,
        row_count,
        col_start - rim_cols,
        col_count + 2 * rim_cols,
        total_frames,
        total_cols,
    )

    def split_heads(tensor):
        return jnp.moveaxis(tensor.reshape(-1, heads_dev, HEAD_DIM), 1, 0)

    def merge_heads(tensor, grid_shape):
        return jnp.moveaxis(tensor, 0, 1).reshape(grid_shape + (channels,))

    key_value = jnp.stack([keys, values])
    key_value = with_halo(key_value, (("sa", 1),), rim_time)
    key_value = with_halo(key_value, (("wa", 3),), rim_cols)
    text_key_all, text_value_all = (
        lax.all_gather(text_keys, "sa", axis=0, tiled=True),
        lax.all_gather(text_values, "sa", axis=0, tiled=True),
    )
    query_heads = split_heads(queries)
    grad_heads = split_heads(out_grad)
    key_heads = split_heads(key_value[0])
    value_heads = split_heads(key_value[1])
    text_key_heads = split_heads(text_key_all)
    text_value_heads = split_heads(text_value_all)

    def forward_one(operands):
        query_head, grad_head, key_head, value_head, text_key, text_value, window = operands
        allowed = pair_mask(own_cells, near_cells, window)
        attended_head, log_total = forward_head(
            query_head, key_head, value_head, text_key, text_value, allowed
        )
        row_delta = jnp.sum(
            grad_head.astype(jnp.float32) * attended_head.astype(jnp.float32), axis=1
        )
        return (attended_head, log_total, row_delta)

    attended_heads, log_totals, row_deltas = lax.map(
        forward_one,
        (
            query_heads,
            grad_heads,
            key_heads,
            value_heads,
            text_key_heads,
            text_value_heads,
            window_ext,
        ),
    )
    own_grid = (frames, row_count, col_count)
    attended = merge_heads(attended_heads, own_grid)

    def query_side(operands):
        (
            query_head,
            grad_head,
            log_total,
            row_delta,
            key_head,
            value_head,
            text_key,
            text_value,
            window,
        ) = operands
        allowed = pair_mask(own_cells, near_cells, window)
        terms = grads_head(
            query_head,
            grad_head,
            log_total,
            row_delta,
            key_head,
            value_head,
            text_key,
            text_value,
            allowed,
        )
        return (terms[0].astype(jnp.bfloat16), terms[3], terms[4])

    query_terms, text_key_terms, text_value_terms = lax.map(
        query_side,
        (
            query_heads,
            grad_heads,
            log_totals,
            row_deltas,
            key_heads,
            value_heads,
            text_key_heads,
            text_value_heads,
            window_ext,
        ),
    )
    query_cot = jnp.stack([queries, out_grad])
    query_cot = with_halo(query_cot, (("sa", 1),), rim_time)
    query_cot = with_halo(query_cot, (("wa", 3),), rim_cols)
    row_stats = jnp.stack([log_totals, row_deltas]).reshape(
        2, heads_dev, frames, row_count, col_count
    )
    row_stats = with_halo(row_stats, (("sa", 2),), rim_time)
    row_stats = with_halo(row_stats, (("wa", 4),), rim_cols)
    row_stats = row_stats.reshape(2, heads_dev, -1)

    def key_side(operands):
        (
            query_head,
            grad_head,
            log_total,
            row_delta,
            key_head,
            value_head,
            text_key,
            text_value,
            window,
        ) = operands
        allowed = pair_mask(near_cells, own_cells, window)
        terms = grads_head(
            query_head,
            grad_head,
            log_total,
            row_delta,
            key_head,
            value_head,
            text_key,
            text_value,
            allowed,
        )
        return (terms[1].astype(jnp.bfloat16), terms[2].astype(jnp.bfloat16))

    key_terms, value_terms = lax.map(
        key_side,
        (
            split_heads(query_cot[0]),
            split_heads(query_cot[1]),
            row_stats[0],
            row_stats[1],
            split_heads(keys),
            split_heads(values),
            text_key_heads,
            text_value_heads,
            window_ext,
        ),
    )
    key_grad = merge_heads(key_terms, own_grid)
    value_grad = merge_heads(value_terms, own_grid)
    query_grad = merge_heads(query_terms, own_grid)
    text_key_sum = jnp.moveaxis(text_key_terms, 0, 1).reshape(-1, channels)
    text_value_sum = jnp.moveaxis(text_value_terms, 0, 1).reshape(-1, channels)
    whole_key, whole_value = lax.psum((text_key_sum, text_value_sum), ("sa", "wa"))
    text_rows_dev = text_keys.shape[0]
    row_start = lax.axis_index("sa") * text_rows_dev
    text_key_grad = lax.dynamic_slice_in_dim(whole_key, row_start, text_rows_dev, 0)
    text_value_grad = lax.dynamic_slice_in_dim(whole_value, row_start, text_rows_dev, 0)
    return (attended, query_grad, key_grad, value_grad, text_key_grad, text_value_grad)


def solution(mesh):
    placed = (
        P(("clips", "sa"), None, "wa", "hp"),
        P(("clips", "sa"), None, "wa", "hp"),
        P(("clips", "sa"), None, "wa", "hp"),
        P(("clips", "sa"), "hp"),
        P(("clips", "sa"), "hp"),
        P(("clips", "sa"), None, "wa", "hp"),
        P("hp", None),
    )
    return jax.shard_map(
        shards,
        mesh=mesh,
        in_specs=placed,
        out_specs=(
            P(("clips", "sa"), None, "wa", "hp"),
            P(("clips", "sa"), None, "wa", "hp"),
            P(("clips", "sa"), None, "wa", "hp"),
            P(("clips", "sa"), None, "wa", "hp"),
            P(("clips", "sa"), "hp"),
            P(("clips", "sa"), "hp"),
        ),
        check_vma=False,
    )
```

profile of v0, /device:TPU:0, one launch (start us, length us, event | category | flops | bytes accessed | tf_op | source)
XLA Modules:
  0.0 626.3 jit_solution(7425015172053281187)
XLA Ops:
  8.5 5.1 collective-permute-start
  14.9 15.4 %collective-permute-done = bf16[2,2,8,8,1536]{4,3,2,1,0:T(8,128)(2,1)S(1)} collective-permute-done((bf16[2,2,8,8,1536]{4,3,2,1,0:T(8,128)(2,1)S(1)}, bf16[2,2,8,8,1536]{4,3,2,1,0:T(8,128)(2,1)S(1)}, u32[]{:S(2)}, u32[]{:S(2)}) %collective-permute-start) | collective-permute-done | bytes 786464 | tf_op jit(solution)/shard_map/ppermute | solution.py:21
  30.4 4.2 collective-permute-done.1
  37.6 5.0 collective-permute-start.2
  49.7 34.4 %all_gather.6 = bf16[256,1536]{1,0:T(8,128)(2,1)} all-gather(bf16[64,1536]{1,0:T(8,128)(2,1)S(1)} %copy-done.22), channel_id=1, replica_groups=mesh['clips'=2,'sa'=4,'wa'=2,'hp'=2] {'sa'}, dimensions={0}, use_global_device_ids=true | all-gather | bytes 983040 | tf_op jit(solution)/shard_map/all_gather | solution.py:130
  92.6 18.7 %all_gather.7 = bf16[256,1536]{1,0:T(8,128)(2,1)} all-gather(bf16[64,1536]{1,0:T(8,128)(2,1)} %param.17), channel_id=1, replica_groups=mesh['clips'=2,'sa'=4,'wa'=2,'hp'=2] {'sa'}, dimensions={0}, use_global_device_ids=true | all-gather | bytes 983040 | tf_op jit(solution)/shard_map/all_gather | solution.py:131
  123.3 6.9 %collective-permute-start.6 = (bf16[2,6,8,8,1536]{4,3,2,1,0:T(8,128)(2,1)}, bf16[2,6,8,8,1536]{4,3,2,1,0:T(8,128)(2,1)}, u32[]{:S(2)}, u32[]{:S(2)}) collective-permute-start(bf16[2,6,8,8,1536]{4,3,2,1,0:T(8,128)(2,1)} %pad_maximum_fusion.3), channel_id=1, source_target_pairs={{0,2},{1,3},{4,6},{5,7},{8,10},{9,11},{12,14},{13,15},{16,18},{17,... | collective-permute-start | bytes 7077896 | tf_op jit(solution)/shard_map/ppermute | solution.py:21
  131.6 3.7 pad_maximum_fusion
  137.8 7.4 %reshape_squeeze.12 = bf16[1152,12,128]{2,1,0:T(8,128)(2,1)} reshape(bf16[1,6,8,24,1536]{4,3,2,1,0:T(8,128)(2,1)} %get-tuple-element.872) | data formatting | bytes 7077888 | tf_op jit(solution)/shard_map/reshape;squeeze | solution.py:121
  145.2 5.1 copy.52
  150.3 4.3 reshape_squeeze.13
  154.6 5.0 copy.54
  159.7 119.1 %while.46 = (s32[]{:T(128)}, bf16[12,128,128]{1,2,0:T(8,128)(2,1)S(1)}, f32[12,128]{1,0:T(8,128)S(1)}, f32[12,128]{1,0:T(8,128)S(1)}, s32[12,3]{0,1:T(4,128)S(1)...) while((s32[]{:T(128)}, ...), condition=%wide.region_6.7_spmd.clone.clone, body=%wide.region_0.6_spmd.clone.clone.sunk | while | flops 95585024 | bytes 3331965 | solution.py:151
  161.1 3.6 fusion.245
  171.0 3.6 fusion.245
  181.0 3.6 fusion.245
  190.9 3.6 fusion.245
  200.8 3.6 fusion.245
  210.7 3.6 fusion.245
  220.7 3.6 fusion.245
  230.6 3.6 fusion.245
  240.5 3.6 fusion.245
  250.5 3.6 fusion.245
  260.4 3.6 fusion.245
  270.3 3.6 fusion.245
  282.6 153.8 %while.47 = (s32[]{:T(128)}, bf16[12,128,128]{2,1,0:T(8,128)(2,1)S(1)}, f32[12,256,128]{1,2,0:T(8,128)}, f32[12,256,128]{1,2,0:T(8,128)}, s32[12,3]{0,1:T(4,128)...) while((s32[]{:T(128)}, ...), condition=%wide.region_8.9_spmd.clone.clone, body=%wide.region_7.8_spmd.clone.clone.sunk | while | flops 158467072 | bytes 3592061 | solution.py:192
  351.8 3.6 fusion.266
  436.5 6.0 pad_maximum_fusion.1
  444.0 6.7 %collective-permute-start.10 = (f32[2,12,6,8,8]{1,4,3,2,0:T(8,128)}, f32[2,12,6,8,8]{1,4,3,2,0:T(8,128)}, u32[]{:S(2)}, u32[]{:S(2)}) collective-permute-start(f32[2,12,6,8,8]{1,4,3,2,0:T(8,128)} %copy.65), channel_id=1, source_target_pairs={{0,2},{1,3},{4,6},{5,7},{8,10},{9,11},{12,14},{13,15},{16,18},{17,... | collective-permute-start | bytes 110600 | tf_op jit(solution)/shard_map/ppermute | solution.py:21
  451.9 5.6 fusion.197
  457.6 7.4 %reshape_squeeze.14 = bf16[1152,12,128]{2,1,0:T(8,128)(2,1)} reshape(bf16[1,6,8,24,1536]{4,3,2,1,0:T(8,128)(2,1)} %get-tuple-element.870) | data formatting | bytes 7077888 | tf_op jit(solution)/shard_map/reshape;squeeze | solution.py:121
  464.9 5.1 copy.69
  470.0 4.3 reshape_squeeze.15
  474.3 5.1 copy.71
  486.6 110.5 %while.48 = (s32[]{:T(128)}, bf16[12,128,128]{2,1,0:T(8,128)(2,1)S(1)}, bf16[12,128,128]{2,1,0:T(8,128)(2,1)S(1)}, s32[12,3]{0,1:T(4,128)S(1)}, bf16[12,1152,128...) while((s32[]{:T(128)}, ...), condition=%wide.region_10.11_spmd.clone.clone, body=%wide.region_9.10_spmd.clone.clone.sunk | while | flops 154190848 | bytes 3222373 | solution.py:242
  488.1 4.9 fusion.281
  497.3 4.8 fusion.281
  506.5 4.8 fusion.281
  515.7 4.8 fusion.281
  524.9 4.8 fusion.281
  534.1 4.8 fusion.281
  543.3 4.8 fusion.281
  552.5 4.8 fusion.281
  561.7 4.8 fusion.281
  570.9 4.8 fusion.281
  580.2 4.8 fusion.281
  589.4 4.8 fusion.281
  599.7 15.9 %all-reduce.3.cloned.1.call-done = (f32[256,1536]{0,1:T(8,128)}, f32[256,1536]{0,1:T(8,128)}) async-done(((f32[256,1536]{0,1:T(8,128)}, f32[256,1536]{0,1:T(8,128)}), (f32[256,1536]{0,1:T(8,128)}, f32[256,1536]{0,1:T(8,128)})) %all-reduce.3.cloned.1.call-update) | async-done | bytes 3145744 | tf_op jit(solution)/shard_map/psum | solution.py:261
  (1100 shorter events, 330.3 us)
Async XLA Ops:
  7.2 36.7 %copy-start.2 = (bf16[2,8,8,1536]{3,2,1,0:T(8,128)(2,1)S(1)}, bf16[2,8,8,1536]{3,2,1,0:T(8,128)(2,1)}, u32[]{:S(2)}) copy-start(bf16[2,8,8,1536]{3,2,1,0:T(8,128)(2,1)} %param.13) | copy-start | bytes 1179652
  7.2 36.7 %copy-start.4 = (bf16[2,8,8,1536]{3,2,1,0:T(8,128)(2,1)S(1)}, bf16[2,8,8,1536]{3,2,1,0:T(8,128)(2,1)}, u32[]{:S(2)}) copy-start(bf16[2,8,8,1536]{3,2,1,0:T(8,128)(2,1)} %param.18) | copy-start | bytes 1179652
  7.2 608.4 %all-reduce.3.cloned.1.call-start = ((), (), s32[]{:S(2)}) async-start(), calls=%async_computation | async-start | bytes 6291456 | tf_op jit(solution)/shard_map/psum | solution.py:261
  8.5 41.2 %copy-start.22 = (bf16[64,1536]{1,0:T(8,128)(2,1)S(1)}, bf16[64,1536]{1,0:T(8,128)(2,1)}, u32[]{:S(2)}) copy-start(bf16[64,1536]{1,0:T(8,128)(2,1)} %param.16) | copy-start | bytes 589828
  8.5 21.9 %collective-permute-start = (bf16[2,2,8,8,1536]{4,3,2,1,0:T(8,128)(2,1)S(1)}, bf16[2,2,8,8,1536]{4,3,2,1,0:T(8,128)(2,1)S(1)}, u32[]{:S(2)}, u32[]{:S(2)}) collective-permute-start(bf16[2,2,8,8,1536]{4,3,2,1,0:T(8,128)(2,1)S(1)} %pad_maximum_fusion.4), channel_id=1, source_target_pairs={{0,4},{4,8},{8,12},{1,5},{5,9},{9,13},{2,6},{6,10},{10,14},{3,7},{... | collective-permute-start | bytes 2359304 | tf_op jit(solution)/shard_map/ppermute | solution.py:21
  13.6 20.9 %collective-permute-start.1 = (bf16[2,2,8,8,1536]{4,3,2,1,0:T(8,128)(2,1)S(1)}, bf16[2,2,8,8,1536]{4,3,2,1,0:T(8,128)(2,1)S(1)}, u32[]{:S(2)}, u32[]{:S(2)}) collective-permute-start(bf16[2,2,8,8,1536]{4,3,2,1,0:T(8,128)(2,1)S(1)} %pad_maximum_fusion.4), channel_id=1, source_target_pairs={{4,0},{8,4},{12,8},{5,1},{9,5},{13,9},{6,2},{10,6},{14,10},{7,3},{... | collective-permute-start | bytes 2359304 | tf_op jit(solution)/shard_map/ppermute | solution.py:22
  30.4 53.7 %copy-start.8 = (bf16[2,2,8,8,1536]{4,3,2,1,0:T(8,128)(2,1)}, bf16[2,2,8,8,1536]{4,3,2,1,0:T(8,128)(2,1)S(1)}, u32[]{:S(2)}) copy-start(bf16[2,2,8,8,1536]{4,3,2,1,0:T(8,128)(2,1)S(1)} %collective-permute-done) | copy-start | bytes 2359300
  34.5 49.5 %copy-start.9 = (bf16[2,2,8,8,1536]{4,3,2,1,0:T(8,128)(2,1)}, bf16[2,2,8,8,1536]{4,3,2,1,0:T(8,128)(2,1)S(1)}, u32[]{:S(2)}) copy-start(bf16[2,2,8,8,1536]{4,3,2,1,0:T(8,128)(2,1)S(1)} %collective-permute-done.1) | copy-start | bytes 2359300
  37.6 49.0 %copy-start.1 = (bf16[2,8,8,1536]{3,2,1,0:T(8,128)(2,1)S(1)}, bf16[2,8,8,1536]{3,2,1,0:T(8,128)(2,1)}, u32[]{:S(2)}) copy-start(bf16[2,8,8,1536]{3,2,1,0:T(8,128)(2,1)} %param.14) | copy-start | bytes 1179652
  37.6 93.9 %collective-permute-start.2 = (bf16[2,6,8,8,1536]{4,3,2,1,0:T(8,128)(2,1)}, bf16[2,6,8,8,1536]{4,3,2,1,0:T(8,128)(2,1)}, u32[]{:S(2)}, u32[]{:S(2)}) collective-permute-start(bf16[2,6,8,8,1536]{4,3,2,1,0:T(8,128)(2,1)} %pad_maximum_fusion.2), channel_id=1, source_target_pairs={{0,2},{1,3},{4,6},{5,7},{8,10},{9,11},{12,14},{13,15},{16,18},{17,... | collective-permute-start | bytes 7077896 | tf_op jit(solution)/shard_map/ppermute | solution.py:21
  42.6 89.0 %collective-permute-start.3 = (bf16[2,6,8,8,1536]{4,3,2,1,0:T(8,128)(2,1)}, bf16[2,6,8,8,1536]{4,3,2,1,0:T(8,128)(2,1)}, u32[]{:S(2)}, u32[]{:S(2)}) collective-permute-start(bf16[2,6,8,8,1536]{4,3,2,1,0:T(8,128)(2,1)} %pad_maximum_fusion.2), channel_id=1, source_target_pairs={{2,0},{3,1},{6,4},{7,5},{10,8},{11,9},{14,12},{15,13},{18,16},{19,... | collective-permute-start | bytes 7077896 | tf_op jit(solution)/shard_map/ppermute | solution.py:22
  43.9 43.8 %copy-start = (bf16[2,8,8,1536]{3,2,1,0:T(8,128)(2,1)S(1)}, bf16[2,8,8,1536]{3,2,1,0:T(8,128)(2,1)}, u32[]{:S(2)}) copy-start(bf16[2,8,8,1536]{3,2,1,0:T(8,128)(2,1)} %param.15) | copy-start | bytes 1179652
  44.9 75.3 %collective-permute-start.4 = (bf16[2,2,8,8,1536]{4,3,2,1,0:T(8,128)(2,1)}, bf16[2,2,8,8,1536]{4,3,2,1,0:T(8,128)(2,1)S(1)}, u32[]{:S(2)}, u32[]{:S(2)}) collective-permute-start(bf16[2,2,8,8,1536]{4,3,2,1,0:T(8,128)(2,1)} %pad_maximum_fusion.5), channel_id=1, source_target_pairs={{0,4},{4,8},{8,12},{1,5},{5,9},{9,13},{2,6},{6,10},{10,14},{3,7},{... | collective-permute-start | bytes 2359304 | tf_op jit(solution)/shard_map/ppermute | solution.py:21
  48.3 71.9 %collective-permute-start.5 = (bf16[2,2,8,8,1536]{4,3,2,1,0:T(8,128)(2,1)}, bf16[2,2,8,8,1536]{4,3,2,1,0:T(8,128)(2,1)}, u32[]{:S(2)}, u32[]{:S(2)}) collective-permute-start(bf16[2,2,8,8,1536]{4,3,2,1,0:T(8,128)(2,1)} %pad_maximum_fusion.5), channel_id=1, source_target_pairs={{4,0},{8,4},{12,8},{5,1},{9,5},{13,9},{6,2},{10,6},{14,10},{7,3},{... | collective-permute-start | bytes 2359304 | tf_op jit(solution)/shard_map/ppermute | solution.py:22
  120.2 11.4 %copy-start.6 = (bf16[2,2,8,8,1536]{4,3,2,1,0:T(8,128)(2,1)}, bf16[2,2,8,8,1536]{4,3,2,1,0:T(8,128)(2,1)S(1)}, u32[]{:S(2)}) copy-start(bf16[2,2,8,8,1536]{4,3,2,1,0:T(8,128)(2,1)S(1)} %collective-permute-done.4) | copy-start | bytes 2359300
  123.3 313.1 %collective-permute-start.6 = (bf16[2,6,8,8,1536]{4,3,2,1,0:T(8,128)(2,1)}, bf16[2,6,8,8,1536]{4,3,2,1,0:T(8,128)(2,1)}, u32[]{:S(2)}, u32[]{:S(2)}) collective-permute-start(bf16[2,6,8,8,1536]{4,3,2,1,0:T(8,128)(2,1)} %pad_maximum_fusion.3), channel_id=1, source_target_pairs={{0,2},{1,3},{4,6},{5,7},{8,10},{9,11},{12,14},{13,15},{16,18},{17,... | collective-permute-start | bytes 7077896 | tf_op jit(solution)/shard_map/ppermute | solution.py:21
  130.3 306.2 %collective-permute-start.7 = (bf16[2,6,8,8,1536]{4,3,2,1,0:T(8,128)(2,1)}, bf16[2,6,8,8,1536]{4,3,2,1,0:T(8,128)(2,1)}, u32[]{:S(2)}, u32[]{:S(2)}) collective-permute-start(bf16[2,6,8,8,1536]{4,3,2,1,0:T(8,128)(2,1)} %pad_maximum_fusion.3), channel_id=1, source_target_pairs={{2,0},{3,1},{6,4},{7,5},{10,8},{11,9},{14,12},{15,13},{18,16},{19,... | collective-permute-start | bytes 7077896 | tf_op jit(solution)/shard_map/ppermute | solution.py:22
  154.6 5.1 copy-start.18
  154.6 5.1 copy-start.19
  154.6 5.1 copy-start.23
  154.6 5.1 copy-start.26
  154.6 5.1 copy-start.27
  278.8 3.8 copy-start.20
  279.1 163.4 %copy-start.12 = (f32[2,12,2,8,8]{4,3,2,1,0:T(8,128)}, f32[2,12,2,8,8]{4,3,2,1,0:T(8,128)S(1)}, u32[]{:S(2)}) copy-start(f32[2,12,2,8,8]{4,3,2,1,0:T(8,128)S(1)} %constant_dynamic-update-slice_fusion) | copy-start | bytes 36868
  279.1 163.4 %collective-permute-start.8 = (f32[2,12,2,8,8]{4,3,2,1,0:T(8,128)S(1)}, f32[2,12,2,8,8]{4,3,2,1,0:T(8,128)S(1)}, u32[]{:S(2)}, u32[]{:S(2)}) collective-permute-start(f32[2,12,2,8,8]{4,3,2,1,0:T(8,128)S(1)} %constant_dynamic-update-slice_fusion), channel_id=1, source_target_pairs={{0,4},{4,8},{8,12},{1,5},{5,9},{9,13},{2,6},{6,10},{10,14},{3,7},{... | collective-permute-start | bytes 36872 | tf_op jit(solution)/shard_map/ppermute | solution.py:21
  281.0 161.5 %collective-permute-start.9 = (f32[2,12,2,8,8]{4,3,2,1,0:T(8,128)S(1)}, f32[2,12,2,8,8]{4,3,2,1,0:T(8,128)S(1)}, u32[]{:S(2)}, u32[]{:S(2)}) collective-permute-start(f32[2,12,2,8,8]{4,3,2,1,0:T(8,128)S(1)} %constant_dynamic-update-slice_fusion), channel_id=1, source_target_pairs={{4,0},{8,4},{12,8},{5,1},{9,5},{13,9},{6,2},{10,6},{14,10},{7,3},{... | collective-permute-start | bytes 36872 | tf_op jit(solution)/shard_map/ppermute | solution.py:22
  282.5 153.9 %copy-start.3 = (bf16[2,8,8,1536]{3,2,1,0:T(8,128)(2,1)S(1)}, bf16[2,8,8,1536]{3,2,1,0:T(8,128)(2,1)}, u32[]{:S(2)}) copy-start(bf16[2,8,8,1536]{3,2,1,0:T(8,128)(2,1)} %param.13) | copy-start | bytes 1179652
  282.5 153.9 %copy-start.5 = (bf16[2,8,8,1536]{3,2,1,0:T(8,128)(2,1)S(1)}, bf16[2,8,8,1536]{3,2,1,0:T(8,128)(2,1)}, u32[]{:S(2)}) copy-start(bf16[2,8,8,1536]{3,2,1,0:T(8,128)(2,1)} %param.18) | copy-start | bytes 1179652
  282.6 153.9 %copy-start.7 = (bf16[2,2,8,8,1536]{4,3,2,1,0:T(8,128)(2,1)S(1)}, bf16[2,2,8,8,1536]{4,3,2,1,0:T(8,128)(2,1)}, u32[]{:S(2)}) copy-start(bf16[2,2,8,8,1536]{4,3,2,1,0:T(8,128)(2,1)} %copy-done.6) | copy-start | bytes 2359300
  436.4 6.1 copy-start.10
  436.4 6.1 copy-start.24
  442.5 8.2 %copy-start.14 = (f32[2,12,2,8,8]{4,3,2,1,0:T(8,128)}, f32[2,12,2,8,8]{4,3,2,1,0:T(8,128)S(1)}, u32[]{:S(2)}) copy-start(f32[2,12,2,8,8]{4,3,2,1,0:T(8,128)S(1)} %collective-permute-done.8) | copy-start | bytes 36868
  442.5 8.1 %copy-start.16 = (f32[2,12,2,8,8]{4,3,2,1,0:T(8,128)}, f32[2,12,2,8,8]{4,3,2,1,0:T(8,128)S(1)}, u32[]{:S(2)}) copy-start(f32[2,12,2,8,8]{4,3,2,1,0:T(8,128)S(1)} %collective-permute-done.9) | copy-start | bytes 36868
  444.0 38.2 %collective-permute-start.10 = (f32[2,12,6,8,8]{1,4,3,2,0:T(8,128)}, f32[2,12,6,8,8]{1,4,3,2,0:T(8,128)}, u32[]{:S(2)}, u32[]{:S(2)}) collective-permute-start(f32[2,12,6,8,8]{1,4,3,2,0:T(8,128)} %copy.65), channel_id=1, source_target_pairs={{0,2},{1,3},{4,6},{5,7},{8,10},{9,11},{12,14},{13,15},{16,18},{17,... | collective-permute-start | bytes 110600 | tf_op jit(solution)/shard_map/ppermute | solution.py:21
  450.7 33.3 %collective-permute-start.11 = (f32[2,12,6,8,8]{1,4,3,2,0:T(8,128)}, f32[2,12,6,8,8]{1,4,3,2,0:T(8,128)}, u32[]{:S(2)}, u32[]{:S(2)}) collective-permute-start(f32[2,12,6,8,8]{1,4,3,2,0:T(8,128)} %copy.65), channel_id=1, source_target_pairs={{2,0},{3,1},{6,4},{7,5},{10,8},{11,9},{14,12},{15,13},{18,16},{19,... | collective-permute-start | bytes 110600 | tf_op jit(solution)/shard_map/ppermute | solution.py:22
  474.3 5.1 copy-start.11
  474.3 6.4 %copy-start.21 = (bf16[12,128,128]{1,2,0:T(8,128)(2,1)S(1)}, bf16[12,128,128]{1,2,0:T(8,128)(2,1)}, u32[]{:S(2)}) copy-start(bf16[12,128,128]{1,2,0:T(8,128)(2,1)} %copy-done.20) | copy-start | bytes 1179652
  480.7 4.9 copy-start.13
  480.7 5.0 copy-start.15
  480.7 5.0 copy-start.17
  482.2 4.4 copy-start.25
Sparse Core Ops, SparseCore 0:
  482.3 133.2 all-reduce.2
where the time goes:
time: 637 us; the launch traced here: 626 us
  matrix products  315 us (49%)
  local copies, waits for them, and re-layouts  130 us (20%)
  blocking collectives  53.1 us (8%)
  starting transfers between devices  37 us (6%)
  other arithmetic  36.3 us (6%)
  waiting for transfers between devices  35.5 us (6%)
  between operations  14.6 us (2%)
    dot_general x24, matrix products, grads_head(): jnp.dot(query_head, key_head.T, preferred_element_type=jnp.float32)  101 us
    dot_general x12, matrix products, forward_head(): jnp.dot(query_head, key_head.T, preferred_element_type=jnp.float32)  43.5 us
    all_gather x1, blocking collectives, shards(): lax.all_gather(text_keys, 'sa', axis=0, tiled=True)  34.4 us
    unnamed x70, local copies, waits for them, and re-layouts  32.6 us
    ppermute x6, starting transfers between devices, with_halo(): before = lax.ppermute(last, axis, up)  29.1 us
    another operation x4, local copies, waits for them, and re-layouts, split_heads(): return jnp.moveaxis(tensor.reshape(-1, heads_dev, HEAD_DIM), 1, 0)  23.4 us
    dot_general x12, matrix products, grads_head(): jnp.dot(text_probs.astype(jnp.bfloat16).T, grad_head, preferred_element_t...  19.6 us
    dot_general x12, matrix products, grads_head(): jnp.dot(text_dscores.T, query_head, preferred_element_type=jnp.float32)  19.6 us
  transfers between devices with their start and end apart: 13, of which 3 were waited for; matrix products, arithmetic and copies ran while one was open for 75% of the time, Pallas kernels for 0%

commit v1 on v0

v1 whole, which is shorter than its diff:
```python
import functools

import jax
import jax.numpy as jnp
from jax import lax
from jax.experimental import pallas as pl
from jax.experimental.pallas import tpu as pltpu
from jax.sharding import PartitionSpec as P

HEAD_DIM = 128
NEG = -1e30
MESH = pl.DeviceIdType.MESH
F32 = jnp.float32
BF16 = jnp.bfloat16
KEY_BLOCK = 256
LOOKAHEAD = 2
LAG = 2


def dot_nt(a, b):
    return lax.dot_general(a, b, (((1,), (1,)), ((), ())), preferred_element_type=F32)


def dot_tn(a, b):
    return lax.dot_general(a, b, (((0,), (0,)), ((), ())), preferred_element_type=F32)


def kernel(
    n_sa, n_wa, heads, cells, text_rows,
    window, q_in, k_in, v_in, g_in, tk_in, tv_in,
    o_out, dq_out, dk_out, dv_out, dtk_out, dtv_out,
    kv, qg, oq, own_part, z_part, z_got, fin, t_part, t_got, t_fin, st, wb, db,
    x_send, x_recv, x_loc, t_send, t_recv, t_loc, z_send, z_recv,
    r_send, r_recv, y_send, y_recv, y_loc, g_send, g_recv, f_send, f_recv,
):
    s = lax.axis_index("sa")
    w = lax.axis_index("wa")
    slab = n_wa * cells
    text = n_sa * text_rows
    text_base = 3 * slab
    n_keys = text_base + text
    scale = HEAD_DIM ** (-0.5)
    has_prev, has_next = s > 0, s < n_sa - 1

    def cols(group, h):
        return pl.ds(pl.multiple_of((group * heads + h) * HEAD_DIM, HEAD_DIM), HEAD_DIM)

    def rows_of(base, index, size):
        return pl.ds(pl.multiple_of(base + index * size, 16), size)

    def remote(src, dst, send, recv, **where):
        return pltpu.make_async_remote_copy(
            src_ref=src, dst_ref=dst, send_sem=send, recv_sem=recv,
            device_id=where, device_id_type=MESH,
        )

    barrier = pltpu.get_barrier_semaphore()
    for d in range(1, n_wa):
        pl.semaphore_signal(barrier, inc=1, device_id={"wa": lax.rem(w + d, n_wa)}, device_id_type=MESH)
    for e in range(1, n_sa):
        pl.semaphore_signal(barrier, inc=1, device_id={"sa": lax.rem(s + e, n_sa)}, device_id_type=MESH)
    pl.semaphore_wait(barrier, n_wa + n_sa - 2)

    ins = (k_in, v_in, q_in, g_in)

    def x_slot(kind, h, source):
        if kind < 2:
            return kv.at[h, kind, rows_of(slab, source, cells)]
        return qg.at[h, kind - 2, rows_of(0, source, cells)]

    def x_copy(kind, h, d, source):
        peer = lax.rem(w + d, n_wa)
        return remote(
            ins[kind].at[:, cols(peer, h)], x_slot(kind, h, source),
            x_send.at[d - 1, h, kind], x_recv.at[d - 1, h, kind], wa=peer,
        )

    def x_local(kind, h):
        return pltpu.make_async_copy(ins[kind].at[:, cols(w, h)], x_slot(kind, h, w), x_loc.at[h, kind])

    def x_wait(kind, h):
        x_local(kind, h).wait()
        for d in range(1, n_wa):
            x_copy(kind, h, d, lax.rem(w + n_wa - d, n_wa)).wait_recv()

    texts = (tk_in, tv_in)

    def t_slot(kind, h, source):
        return kv.at[h, kind, rows_of(text_base, source, text_rows)]

    def t_copy(kind, h, e, source):
        return remote(
            texts[kind].at[:, cols(w, h)], t_slot(kind, h, source),
            t_send.at[e - 1, h, kind], t_recv.at[e - 1, h, kind], sa=lax.rem(s + e, n_sa),
        )

    def t_local(kind, h):
        return pltpu.make_async_copy(texts[kind].at[:, cols(w, h)], t_slot(kind, h, s), t_loc.at[h, kind])

    def z_copy(side, h):
        target = lax.rem(s + 1, n_sa) if side == 0 else lax.rem(s + n_sa - 1, n_sa)
        return remote(
            kv.at[h, :, pl.ds(slab, slab)], kv.at[h, :, pl.ds(0 if side == 0 else 2 * slab, slab)],
            z_send.at[side, h], z_recv.at[side, h], sa=target,
        )

    def r_copy(side, h):
        target = lax.rem(s + n_sa - 1, n_sa) if side == 0 else lax.rem(s + 1, n_sa)
        return remote(
            z_part.at[side, h], z_got.at[side, h], r_send.at[side, h], r_recv.at[side, h], sa=target,
        )

    @pl.when(jnp.logical_not(has_prev))
    def _():
        def clear(h, c):
            kv[h, :, pl.ds(0, slab)] = jnp.zeros((2, slab, HEAD_DIM), BF16)
            z_got[1, h] = jnp.zeros((2, slab, HEAD_DIM), BF16)
            return c

        lax.fori_loop(0, heads, clear, 0)

    @pl.when(jnp.logical_not(has_next))
    def _():
        def clear(h, c):
            kv[h, :, pl.ds(2 * slab, slab)] = jnp.zeros((2, slab, HEAD_DIM), BF16)
            z_got[0, h] = jnp.zeros((2, slab, HEAD_DIM), BF16)
            return c

        lax.fori_loop(0, heads, clear, 0)

    def open_head(h, c):
        for kind in range(4):
            for d in range(1, n_wa):
                x_copy(kind, h, d, w).start()
            x_local(kind, h).start()
        return c

    lax.fori_loop(0, heads, open_head, 0)

    def feed(h):
        for kind in range(2):
            for e in range(1, n_sa):
                t_copy(kind, h, e, s).start()
            t_local(kind, h).start()
        x_wait(0, h)
        x_wait(1, h)

        @pl.when(has_next)
        def _():
            z_copy(0, h).start()

        @pl.when(has_prev)
        def _():
            z_copy(1, h).start()

    for h in range(min(LOOKAHEAD, heads)):
        feed(h)

    q_block = min(slab, 256)

    def compute(h):
        ext_t = window[w * heads + h, 0]
        ext_w = window[w * heads + h, 2]
        near = (
            jnp.logical_and(has_prev, ext_t >= 1),
            None,
            jnp.logical_and(has_next, ext_t >= 1),
        )
        for qb in range(slab // q_block):
            q_rows = pl.ds(qb * q_block, q_block)
            q = qg[h, 0, q_rows]
            g = qg[h, 1, q_rows]
            query_col = qb * (q_block // cells) + lax.broadcasted_iota(jnp.int32, (1, q_block), 1) // cells
            top = jnp.full((1, q_block), NEG, F32)
            blocks = []
            for j in range(3):
                far = 0.0 if near[j] is None else jnp.where(near[j], 0.0, NEG)
                for c in range(n_wa):
                    bias = jnp.where(jnp.abs(query_col - c) <= ext_w, far, NEG)
                    blocks.append(((j * n_wa + c) * cells, cells, bias))
            for b in range(0, text, KEY_BLOCK):
                blocks.append((text_base + b, min(KEY_BLOCK, text - b), None))
            for start, size, bias in blocks:
                sc = dot_nt(kv[h, 0, pl.ds(start, size)], q) * scale
                if bias is not None:
                    sc = sc + bias
                st[pl.ds(start, size)] = sc
                top = jnp.maximum(top, jnp.max(sc, axis=0, keepdims=True))
            total = jnp.zeros((1, q_block), F32)
            for start, size, _ in blocks:
                p = jnp.exp(st[pl.ds(start, size)] - top)
                st[pl.ds(start, size)] = p
                total = total + jnp.sum(p, axis=0, keepdims=True)
            inv = 1.0 / total
            for start, size, _ in blocks:
                wb[pl.ds(start, size)] = (st[pl.ds(start, size)] * inv).astype(BF16)
            attended = dot_tn(wb[...], kv[h, 1]).astype(BF16)
            oq[h, 0, q_rows] = attended
            product = g.astype(F32) * attended.astype(F32)
            delta = jnp.sum(product.T, axis=0, keepdims=True)
            inv_scale = inv * scale
            for start, size, _ in blocks:
                dp = dot_nt(kv[h, 1, pl.ds(start, size)], g)
                db[pl.ds(start, size)] = (st[pl.ds(start, size)] * inv_scale * (dp - delta)).astype(BF16)
            oq[h, 1, q_rows] = dot_tn(db[...], kv[h, 0]).astype(BF16)

            def put(ref, index, value, at):
                if qb == 0:
                    ref[index] = value.astype(ref.dtype)
                else:
                    ref[index] = (ref[index].astype(F32) + value).astype(ref.dtype)

            for kind, (left, right) in enumerate(((db, q), (wb, g))):
                for j in range(3):
                    part = jnp.dot(left[pl.ds(j * slab, slab)], right, preferred_element_type=F32)
                    if j == 1:
                        put(own_part, (h, kind), part, qb)
                    else:
                        put(z_part, (j // 2, h, kind), part, qb)
                part = jnp.dot(left[pl.ds(text_base, text)], right, preferred_element_type=F32)
                put(t_part, (h, kind), part, qb)

    outs = (dk_out, dv_out, o_out, dq_out)

    def y_src(kind, h, owner):
        ref = fin if kind < 2 else oq
        return ref.at[h, kind % 2, rows_of(0, owner, cells)]

    def y_copy(kind, h, d, source):
        peer = lax.rem(w + d, n_wa)
        return remote(
            y_src(kind, h, peer), outs[kind].at[:, cols(source, h)],
            y_send.at[d - 1, h, kind], y_recv.at[d - 1, h, kind], wa=peer,
        )

    def y_local(kind, h):
        return pltpu.make_async_copy(y_src(kind, h, w), outs[kind].at[:, cols(w, h)], y_loc.at[h, kind])

    def y_start(kind, h):
        for d in range(1, n_wa):
            y_copy(kind, h, d, w).start()
        y_local(kind, h).start()

    def g_copy(h, e):
        peer = lax.rem(s + e, n_sa)
        return remote(
            t_part.at[h, :, rows_of(0, peer, text_rows)], t_got.at[e - 1, h],
            g_send.at[e - 1, h], g_recv.at[e - 1, h], sa=peer,
        )

    def f_copy(h, d, source):
        return remote(
            t_fin.at[w, h], t_fin.at[source, h],
            f_send.at[d - 1, h], f_recv.at[d - 1, h], wa=lax.rem(w + d, n_wa),
        )

    def finish(h):
        @pl.when(has_next)
        def _():
            r_copy(0, h).wait_recv()

        @pl.when(has_prev)
        def _():
            r_copy(1, h).wait_recv()

        whole = own_part[h] + z_got[0, h].astype(F32) + z_got[1, h].astype(F32)
        fin[h] = whole.astype(BF16)
        y_start(0, h)
        y_start(1, h)
        whole = t_part[h, :, rows_of(0, s, text_rows)].astype(F32)
        for e in range(1, n_sa):
            g_copy(h, e).wait_recv()
            whole = whole + t_got[e - 1, h].astype(F32)
        t_fin[w, h] = whole.astype(BF16)
        for d in range(1, n_wa):
            f_copy(h, d, w).start()

    def step(h, c):
        @pl.when(h + LOOKAHEAD < heads)
        def _():
            feed(h + LOOKAHEAD)

        x_wait(2, h)
        x_wait(3, h)
        for kind in range(2):
            t_local(kind, h).wait()
            for e in range(1, n_sa):
                t_copy(kind, h, e, lax.rem(s + n_sa - e, n_sa)).wait_recv()

        @pl.when(has_prev)
        def _():
            z_copy(0, h).wait_recv()

        @pl.when(has_next)
        def _():
            z_copy(1, h).wait_recv()

        compute(h)

        @pl.when(has_prev)
        def _():
            r_copy(0, h).start()

        @pl.when(has_next)
        def _():
            r_copy(1, h).start()

        for e in range(1, n_sa):
            g_copy(h, e).start()
        y_start(2, h)
        y_start(3, h)

        @pl.when(h >= LAG)
        def _():
            finish(h - LAG)

        return c

    lax.fori_loop(0, heads, step, 0)

    def tail(h, c):
        finish(h)
        return c

    lax.fori_loop(max(heads - LAG, 0), heads, tail, 0)

    def close(h, c):
        for kind in range(4):
            for d in range(1, n_wa):
                x_copy(kind, h, d, w).wait_send()
                y_copy(kind, h, d, w).wait_send()
                y_copy(kind, h, d, lax.rem(w + n_wa - d, n_wa)).wait_recv()
            y_local(kind, h).wait()
        for e in range(1, n_sa):
            for kind in range(2):
                t_copy(kind, h, e, s).wait_send()
            g_copy(h, e).wait_send()
        for d in range(1, n_wa):
            f_copy(h, d, w).wait_send()
            f_copy(h, d, lax.rem(w + n_wa - d, n_wa)).wait_recv()

        @pl.when(has_next)
        def _():
            z_copy(0, h).wait_send()
            r_copy(1, h).wait_send()

        @pl.when(has_prev)
        def _():
            z_copy(1, h).wait_send()
            r_copy(0, h).wait_send()

        for source in range(n_wa):
            dtk_out[:, cols(source, h)] = t_fin[source, h, 0].astype(F32)
            dtv_out[:, cols(source, h)] = t_fin[source, h, 1].astype(F32)
        return c

    lax.fori_loop(0, heads, close, 0)


def shards(queries, keys, values, text_keys, text_values, out_grad, window_ext):
    n_sa, n_wa = lax.axis_size("sa"), lax.axis_size("wa")
    grid = queries.shape
    channels = grid[-1]
    cells = grid[0] * grid[1] * grid[2]
    heads = channels // HEAD_DIM // n_wa
    text_rows = text_keys.shape[0]
    slab, text = n_wa * cells, n_sa * text_rows
    n_keys = 3 * slab + text
    q_block = min(slab, 256)
    flat = (cells, channels)
    dma = pltpu.SemaphoreType.DMA
    anywhere = pl.BlockSpec(memory_space=pl.ANY)
    in_vmem = pl.BlockSpec(memory_space=pltpu.VMEM)
    cell_out = jax.ShapeDtypeStruct(flat, BF16)
    text_out = jax.ShapeDtypeStruct((text_rows, channels), F32)
    outs = pl.pallas_call(
        functools.partial(kernel, n_sa, n_wa, heads, cells, text_rows),
        out_shape=(cell_out,) * 4 + (text_out,) * 2,
        in_specs=[pl.BlockSpec(memory_space=pltpu.SMEM)] + [anywhere] * 6,
        out_specs=(anywhere,) * 4 + (in_vmem,) * 2,
        scratch_shapes=[
            pltpu.VMEM((heads, 2, n_keys, HEAD_DIM), BF16),
            pltpu.VMEM((heads, 2, slab, HEAD_DIM), BF16),
            pltpu.VMEM((heads, 2, slab, HEAD_DIM), BF16),
            pltpu.VMEM((heads, 2, slab, HEAD_DIM), F32),
            pltpu.VMEM((2, heads, 2, slab, HEAD_DIM), BF16),
            pltpu.VMEM((2, heads, 2, slab, HEAD_DIM), BF16),
            pltpu.VMEM((heads, 2, slab, HEAD_DIM), BF16),
            pltpu.VMEM((heads, 2, text, HEAD_DIM), BF16),
            pltpu.VMEM((n_sa - 1, heads, 2, text_rows, HEAD_DIM), BF16),
            pltpu.VMEM((n_wa, heads, 2, text_rows, HEAD_DIM), BF16),
            pltpu.VMEM((n_keys, q_block), F32),
            pltpu.VMEM((n_keys, q_block), BF16),
            pltpu.VMEM((n_keys, q_block), BF16),
            dma((n_wa - 1, heads, 4)),
            dma((n_wa - 1, heads, 4)),
            dma((heads, 4)),
            dma((n_sa - 1, heads, 2)),
            dma((n_sa - 1, heads, 2)),
            dma((heads, 2)),
            dma((2, heads)),
            dma((2, heads)),
            dma((2, heads)),
            dma((2, heads)),
            dma((n_wa - 1, heads, 4)),
            dma((n_wa - 1, heads, 4)),
            dma((heads, 4)),
            dma((n_sa - 1, heads)),
            dma((n_sa - 1, heads)),
            dma((n_wa - 1, heads)),
            dma((n_wa - 1, heads)),
        ],
        compiler_params=pltpu.CompilerParams(
            collective_id=0, has_side_effects=True, vmem_limit_bytes=60 * 1024 * 1024
        ),
    )(
        window_ext, queries.reshape(flat), keys.reshape(flat), values.reshape(flat),
        out_grad.reshape(flat), text_keys, text_values,
    )
    return tuple(out.reshape(grid) for out in outs[:4]) + tuple(outs[4:])


def solution(mesh):
    cell = P(("clips", "sa"), None, "wa", "hp")
    text = P(("clips", "sa"), "hp")
    return jax.shard_map(
        shards,
        mesh=mesh,
        in_specs=(cell, cell, cell, text, text, cell, P("hp", None)),
        out_specs=(cell, cell, cell, cell, text, text),
        check_vma=False,
    )
```

time: 637 us -> 91.2 us (0.14); the launches traced: 626 us -> 90.7 us
  matrix products: 315 us -> 0 us
  local copies, waits for them, and re-layouts: 130 us -> 8.47 us
  Pallas kernels: 0 us -> 81.6 us
  blocking collectives: 53.1 us -> 0 us
  starting transfers between devices: 37 us -> 0 us
  other arithmetic: 36.3 us -> 0 us
  waiting for transfers between devices: 35.5 us -> 0 us
  between operations: 14.6 us -> 0.66 us
    dot_general x168 -> x0, matrix products: 315 us -> none  [the longest x24 101 us: grads_head(): jnp.dot(query_head, key_head.T, preferred_element_type=jnp.float32)]
    pallas_call x0 -> x1, Pallas kernels: none -> 81.6 us  [shards(): pl.pallas_call(functools.partial(kernel, n_sa, n_wa, heads, cells, text_r...]
    all_gather x2 -> x0, blocking collectives: 53.1 us -> none  [the longest x1 34.4 us: shards(): lax.all_gather(text_keys, 'sa', axis=0, tiled=True)]
    ppermute x12 -> x0, starting transfers between devices: 37 us -> none  [the longest x6 29.1 us: with_halo(): before = lax.ppermute(last, axis, up)]
    slice x39 -> x0, local copies, waits for them, and re-layouts: 27 us -> none  [the longest x36 18.8 us: pair_mask(): allowed = allowed & (apart <= window[axis_number])]
    reshape x224 -> x0, local copies, waits for them, and re-layouts: 24.3 us -> none  [the longest x72 6.35 us: tile_coords(): time_grid = jnp.broadcast_to(times[:, None, None], grid_shape).reshape(-1)]
    unnamed x70 -> x19, local copies, waits for them, and re-layouts: 32.6 us -> 8.47 us
    another operation x10 -> x0, local copies, waits for them, and re-layouts: 23.8 us -> none  [the longest x4 23.4 us: split_heads(): return jnp.moveaxis(tensor.reshape(-1, heads_dev, HEAD_DIM), 1, 0)]
  transfers between devices with their start and end apart: 13 -> 0, of which waited for: 3 -> 0; matrix products, arithmetic and copies ran while one was open for 75% -> 0% of each run, Pallas kernels for 0% -> 0%
where the time goes in v1:
time: 91.2 us; the launch traced here: 90.7 us
  Pallas kernels  81.6 us (89%)
  local copies, waits for them, and re-layouts  8.47 us (9%)
    pallas_call x1, Pallas kernels, shards(): pl.pallas_call(functools.partial(kernel, n_sa, n_wa, heads, cells, text_r...  81.6 us
    unnamed x19, local copies, waits for them, and re-layouts  8.47 us

profile of v1, /device:TPU:0, one launch (start us, length us, event | category | flops | bytes accessed | tf_op | source)
XLA Modules:
  0.0 90.7 jit_solution(12839174944774873249)
XLA Ops:
  0.6 0.0 copy-start.5
  0.6 0.7 copy-done.5
  1.3 0.7 copy.13.window
  2.0 81.6 %shard_map.118 = (bf16[128,1536]{1,0:T(8,128)(2,1)}, bf16[128,1536]{1,0:T(8,128)(2,1)}, bf16[128,1536]{1,0:T(8,128)(2,1)}, bf16[128,1536]{1,0:T(8,128)(2,1)}, f32[64,1536]{1,0:T(8,128)}, /*index=5*/f32[64,1536]{1,0:T(8,128)}) custom-call(s32[12,3]{1,0:T(8,128)} %copy.13.window, bf16[128,1536]{1,0:T(8,128)(2,1)} %bitcast.12, bf16[128,1536]{1,0:T(8,128)(2,1)} %bitcast.13, ...), custom_call_target="tpu_custom_call" | custom-call | tf_op jit(solution)/shard_map/pallas_call | solution.py:376
  83.6 0.0 copy-start.4
  83.6 1.8 %copy.20 = bf16[2,8,8,1536]{3,2,1,0:T(8,128)(2,1)} copy(bf16[2,8,8,1536]{3,2,1,0:T(8,128)(2,1)} %bitcast.11) | data formatting | bytes 786432
  85.4 0.0 copy-done.4
  85.4 0.0 copy-start.3
  85.4 0.7 copy.21
  86.2 0.4 copy-done.3
  86.6 0.0 copy-start.2
  86.6 0.7 copy.22
  87.3 0.4 copy-done.2
  87.7 0.0 copy-start.1
  87.7 0.7 copy.23
  88.4 0.4 copy-done.1
  88.8 0.0 copy-start
  88.8 0.7 copy.24
  89.6 0.4 copy-done
  90.0 0.7 copy.25
Async XLA Ops:
  0.6 0.7 copy-start.5
  83.6 1.8 %copy-start.4 = (bf16[128,1536]{1,0:T(8,128)(2,1)S(1)}, bf16[128,1536]{1,0:T(8,128)(2,1)}, u32[]{:S(2)}) copy-start(bf16[128,1536]{1,0:T(8,128)(2,1)} %get-tuple-element.13) | copy-start | bytes 1179652
  85.4 1.1 %copy-start.3 = (bf16[128,1536]{1,0:T(8,128)(2,1)S(1)}, bf16[128,1536]{1,0:T(8,128)(2,1)}, u32[]{:S(2)}) copy-start(bf16[128,1536]{1,0:T(8,128)(2,1)} %get-tuple-element.14) | copy-start | bytes 1179652
  86.6 1.1 %copy-start.2 = (bf16[128,1536]{1,0:T(8,128)(2,1)S(1)}, bf16[128,1536]{1,0:T(8,128)(2,1)}, u32[]{:S(2)}) copy-start(bf16[128,1536]{1,0:T(8,128)(2,1)} %get-tuple-element.15) | copy-start | bytes 1179652
  87.7 1.1 %copy-start.1 = (f32[64,1536]{1,0:T(8,128)S(1)}, f32[64,1536]{1,0:T(8,128)}, u32[]{:S(2)}) copy-start(f32[64,1536]{1,0:T(8,128)} %get-tuple-element.28) | copy-start | bytes 1179652
  88.8 1.1 %copy-start = (f32[64,1536]{1,0:T(8,128)S(1)}, f32[64,1536]{1,0:T(8,128)}, u32[]{:S(2)}) copy-start(f32[64,1536]{1,0:T(8,128)} %get-tuple-element.29) | copy-start | bytes 1179652

commit v2 on v1

--- a/solution.py
+++ b/solution.py
@@ -13,7 +13,7 @@
 F32 = jnp.float32
 BF16 = jnp.bfloat16
 KEY_BLOCK = 256
-LOOKAHEAD = 2
+LOOKAHEAD = 3
 LAG = 2
 
 
@@ -41,6 +41,7 @@
     n_keys = text_base + text
     scale = HEAD_DIM ** (-0.5)
     has_prev, has_next = s > 0, s < n_sa - 1
+    before, after = lax.rem(s + n_sa - 1, n_sa), lax.rem(s + 1, n_sa)
 
     def cols(group, h):
         return pl.ds(pl.multiple_of((group * heads + h) * HEAD_DIM, HEAD_DIM), HEAD_DIM)
@@ -57,9 +58,17 @@
     barrier = pltpu.get_barrier_semaphore()
     for d in range(1, n_wa):
         pl.semaphore_signal(barrier, inc=1, device_id={"wa": lax.rem(w + d, n_wa)}, device_id_type=MESH)
-    for e in range(1, n_sa):
-        pl.semaphore_signal(barrier, inc=1, device_id={"sa": lax.rem(s + e, n_sa)}, device_id_type=MESH)
-    pl.semaphore_wait(barrier, n_wa + n_sa - 2)
+    neighbours = n_wa - 1 + has_prev.astype(jnp.int32) + has_next.astype(jnp.int32)
+
+    @pl.when(has_prev)
+    def _():
+        pl.semaphore_signal(barrier, inc=1, device_id={"sa": before}, device_id_type=MESH)
+
+    @pl.when(has_next)
+    def _():
+        pl.semaphore_signal(barrier, inc=1, device_id={"sa": after}, device_id_type=MESH)
+
+    pl.semaphore_wait(barrier, neighbours)
 
     ins = (k_in, v_in, q_in, g_in)
 
@@ -85,17 +94,39 @@
 
     texts = (tk_in, tv_in)
 
-    def t_slot(kind, h, source):
-        return kv.at[h, kind, rows_of(text_base, source, text_rows)]
-
-    def t_copy(kind, h, e, source):
-        return remote(
-            texts[kind].at[:, cols(w, h)], t_slot(kind, h, source),
-            t_send.at[e - 1, h, kind], t_recv.at[e - 1, h, kind], sa=lax.rem(s + e, n_sa),
-        )
+    def t_slot(h, block):
+        return kv.at[h, :, rows_of(text_base, block, text_rows)]
+
+    def t_hop(side, h, hop, block):
+        return remote(
+            t_slot(h, block), t_slot(h, block), t_send.at[side, h, hop], t_recv.at[side, h, hop],
+            sa=after if side == 0 else before,
+        )
+
+    def t_out(side, h, hop):
+        return t_hop(side, h, hop, s - hop if side == 0 else s + hop)
+
+    def t_in(side, h, hop):
+        return t_hop(side, h, hop, s - 1 - hop if side == 0 else s + 1 + hop)
+
+    def t_valid(side, hop):
+        if side == 0:
+            return jnp.logical_and(s >= hop, has_next)
+        return jnp.logical_and(s + hop < n_sa, has_prev)
 
     def t_local(kind, h):
-        return pltpu.make_async_copy(texts[kind].at[:, cols(w, h)], t_slot(kind, h, s), t_loc.at[h, kind])
+        return pltpu.make_async_copy(
+            texts[kind].at[:, cols(w, h)],
+            kv.at[h, kind, rows_of(text_base, s, text_rows)], t_loc.at[h, kind],
+        )
+
+    def t_forward(h, hop):
+        for side in range(2):
+            @pl.when(t_valid(side, hop))
+            def _():
+                if hop:
+                    t_in(side, h, hop - 1).wait_recv()
+                t_out(side, h, hop).start()
 
     def z_copy(side, h):
         target = lax.rem(s + 1, n_sa) if side == 0 else lax.rem(s + n_sa - 1, n_sa)
@@ -115,6 +146,7 @@
         def clear(h, c):
             kv[h, :, pl.ds(0, slab)] = jnp.zeros((2, slab, HEAD_DIM), BF16)
             z_got[1, h] = jnp.zeros((2, slab, HEAD_DIM), BF16)
+            t_got[0, h, 0] = jnp.zeros((2, text_rows, HEAD_DIM), BF16)
             return c
 
         lax.fori_loop(0, heads, clear, 0)
@@ -124,6 +156,7 @@
         def clear(h, c):
             kv[h, :, pl.ds(2 * slab, slab)] = jnp.zeros((2, slab, HEAD_DIM), BF16)
             z_got[0, h] = jnp.zeros((2, slab, HEAD_DIM), BF16)
+            t_got[1, h, n_sa - 1] = jnp.zeros((2, text_rows, HEAD_DIM), BF16)
             return c
 
         lax.fori_loop(0, heads, clear, 0)
@@ -132,16 +165,23 @@
         for kind in range(4):
             for d in range(1, n_wa):
                 x_copy(kind, h, d, w).start()
+        for kind in range(2):
+            t_local(kind, h).start()
+        for kind in range(4):
             x_local(kind, h).start()
         return c
 
     lax.fori_loop(0, heads, open_head, 0)
 
+    def open_text(h, c):
+        for kind in range(2):
+            t_local(kind, h).wait()
+        t_forward(h, 0)
+        return c
+
+    lax.fori_loop(0, heads, open_text, 0)
+
     def feed(h):
-        for kind in range(2):
-            for e in range(1, n_sa):
-                t_copy(kind, h, e, s).start()
-            t_local(kind, h).start()
         x_wait(0, h)
         x_wait(1, h)
 
@@ -153,14 +193,22 @@
         def _():
             z_copy(1, h).start()
 
+        t_forward(h, 1)
+
+    def feed_text(h):
+        for hop in range(2, n_sa - 1):
+            t_forward(h, hop)
+
     for h in range(min(LOOKAHEAD, heads)):
         feed(h)
+    for h in range(min(LOOKAHEAD - 1, heads)):
+        feed_text(h)
 
     q_block = min(slab, 256)
 
     def compute(h):
-        ext_t = window[w * heads + h, 0]
-        ext_w = window[w * heads + h, 2]
+        ext_t = window[0, w * heads + h]
+        ext_w = window[2, w * heads + h]
         near = (
             jnp.logical_and(has_prev, ext_t >= 1),
             None,
@@ -241,12 +289,29 @@
             y_copy(kind, h, d, w).start()
         y_local(kind, h).start()
 
-    def g_copy(h, e):
-        peer = lax.rem(s + e, n_sa)
-        return remote(
-            t_part.at[h, :, rows_of(0, peer, text_rows)], t_got.at[e - 1, h],
-            g_send.at[e - 1, h], g_recv.at[e - 1, h], sa=peer,
-        )
+    def g_copy(side, h, block):
+        return remote(
+            t_part.at[h, :, rows_of(0, block, text_rows)], t_got.at[side, h, block],
+            g_send.at[side, h, block], g_recv.at[side, h, block],
+            sa=after if side == 0 else before,
+        )
+
+    def g_valid(side, block):
+        return s < block if side == 0 else s > block
+
+    def g_relay(side, h):
+        inward = has_prev if side == 0 else has_next
+        for block in range(n_sa):
+            @pl.when(g_valid(side, block))
+            def _():
+                @pl.when(inward)
+                def _():
+                    g_copy(side, h, block).wait_recv()
+                    rows = pl.ds(block * text_rows, text_rows)
+                    joined = t_part[h, :, rows].astype(F32) + t_got[side, h, block].astype(F32)
+                    t_part[h, :, rows] = joined.astype(BF16)
+
+                g_copy(side, h, block).start()
 
     def f_copy(h, d, source):
         return remote(
@@ -267,25 +332,35 @@
         fin[h] = whole.astype(BF16)
         y_start(0, h)
         y_start(1, h)
+
+    def finish_text(h):
+        @pl.when(has_prev)
+        def _():
+            g_copy(0, h, s).wait_recv()
+
+        @pl.when(has_next)
+        def _():
+            g_copy(1, h, s).wait_recv()
+
         whole = t_part[h, :, rows_of(0, s, text_rows)].astype(F32)
-        for e in range(1, n_sa):
-            g_copy(h, e).wait_recv()
-            whole = whole + t_got[e - 1, h].astype(F32)
+        whole = whole + t_got[0, h, s].astype(F32) + t_got[1, h, s].astype(F32)
         t_fin[w, h] = whole.astype(BF16)
         for d in range(1, n_wa):
             f_copy(h, d, w).start()
 
-    def step(h, c):
-        @pl.when(h + LOOKAHEAD < heads)
-        def _():
-            feed(h + LOOKAHEAD)
-
+    def attend(h):
         x_wait(2, h)
         x_wait(3, h)
-        for kind in range(2):
-            t_local(kind, h).wait()
-            for e in range(1, n_sa):
-                t_copy(kind, h, e, lax.rem(s + n_sa - e, n_sa)).wait_recv()
+
+        @pl.when(jnp.logical_not(has_next))
+        def _():
+            for hop in range(n_sa - 1):
+                t_in(0, h, hop).wait_recv()
+
+        @pl.when(jnp.logical_not(has_prev))
+        def _():
+            for hop in range(n_sa - 1):
+                t_in(1, h, hop).wait_recv()
 
         @pl.when(has_prev)
         def _():
@@ -305,24 +380,40 @@
         def _():
             r_copy(1, h).start()
 
-        for e in range(1, n_sa):
-            g_copy(h, e).start()
         y_start(2, h)
         y_start(3, h)
 
-        @pl.when(h >= LAG)
-        def _():
-            finish(h - LAG)
+    def step(i, c):
+        @pl.when(i + LOOKAHEAD < heads)
+        def _():
+            feed(i + LOOKAHEAD)
+
+        @pl.when(i + LOOKAHEAD - 1 < heads)
+        def _():
+            feed_text(i + LOOKAHEAD - 1)
+
+        @pl.when(i < heads)
+        def _():
+            attend(i)
+
+        for side in range(2):
+            h = i - (s if side == 0 else n_sa - 1 - s)
+
+            @pl.when(jnp.logical_and(h >= 0, h < heads))
+            def _():
+                g_relay(side, h)
+
+        @pl.when(jnp.logical_and(i >= LAG, i < heads + LAG))
+        def _():
+            finish(i - LAG)
+
+        @pl.when(jnp.logical_and(i >= n_sa - 1, i < heads + n_sa - 1))
+        def _():
+            finish_text(i - (n_sa - 1))
 
         return c
 
-    lax.fori_loop(0, heads, step, 0)
-
-    def tail(h, c):
-        finish(h)
-        return c
-
-    lax.fori_loop(max(heads - LAG, 0), heads, tail, 0)
+    lax.fori_loop(0, heads + max(n_sa - 1, LAG), step, 0)
 
     def close(h, c):
         for kind in range(4):
@@ -331,10 +422,17 @@
                 y_copy(kind, h, d, w).wait_send()
                 y_copy(kind, h, d, lax.rem(w + n_wa - d, n_wa)).wait_recv()
             y_local(kind, h).wait()
-        for e in range(1, n_sa):
-            for kind in range(2):
-                t_copy(kind, h, e, s).wait_send()
-            g_copy(h, e).wait_send()
+        for side in range(2):
+            for hop in range(n_sa - 1):
+                @pl.when(t_valid(side, hop))
+                def _():
+                    t_out(side, h, hop).wait_send()
+
+            for block in range(n_sa):
+                @pl.when(g_valid(side, block))
+                def _():
+                    g_copy(side, h, block).wait_send()
+
         for d in range(1, n_wa):
             f_copy(h, d, w).wait_send()
             f_copy(h, d, lax.rem(w + n_wa - d, n_wa)).wait_recv()
@@ -350,11 +448,17 @@
             r_copy(0, h).wait_send()
 
         for source in range(n_wa):
-            dtk_out[:, cols(source, h)] = t_fin[source, h, 0].astype(F32)
-            dtv_out[:, cols(source, h)] = t_fin[source, h, 1].astype(F32)
+            dtk_out[:, cols(source, h)] = t_fin[source, h, 0]
+            dtv_out[:, cols(source, h)] = t_fin[source, h, 1]
         return c
 
     lax.fori_loop(0, heads, close, 0)
+
+
+def hand_over(*refs):
+    half = len(refs) // 2
+    for source, target in zip(refs[:half], refs[half:]):
+        target[...] = source[...].astype(target.dtype)
 
 
 def shards(queries, keys, values, text_keys, text_values, out_grad, window_ext):
@@ -372,7 +476,7 @@
     anywhere = pl.BlockSpec(memory_space=pl.ANY)
     in_vmem = pl.BlockSpec(memory_space=pltpu.VMEM)
     cell_out = jax.ShapeDtypeStruct(flat, BF16)
-    text_out = jax.ShapeDtypeStruct((text_rows, channels), F32)
+    text_out = jax.ShapeDtypeStruct((text_rows, channels), BF16)
     outs = pl.pallas_call(
         functools.partial(kernel, n_sa, n_wa, heads, cells, text_rows),
         out_shape=(cell_out,) * 4 + (text_out,) * 2,
@@ -387,7 +491,7 @@
             pltpu.VMEM((2, heads, 2, slab, HEAD_DIM), BF16),
             pltpu.VMEM((heads, 2, slab, HEAD_DIM), BF16),
             pltpu.VMEM((heads, 2, text, HEAD_DIM), BF16),
-            pltpu.VMEM((n_sa - 1, heads, 2, text_rows, HEAD_DIM), BF16),
+            pltpu.VMEM((2, heads, n_sa, 2, text_rows, HEAD_DIM), BF16),
             pltpu.VMEM((n_wa, heads, 2, text_rows, HEAD_DIM), BF16),
             pltpu.VMEM((n_keys, q_block), F32),
             pltpu.VMEM((n_keys, q_block), BF16),
@@ -395,8 +499,8 @@
             dma((n_wa - 1, heads, 4)),
             dma((n_wa - 1, heads, 4)),
             dma((heads, 4)),
-            dma((n_sa - 1, heads, 2)),
-            dma((n_sa - 1, heads, 2)),
+            dma((2, heads, n_sa - 1)),
+            dma((2, heads, n_sa - 1)),
             dma((heads, 2)),
             dma((2, heads)),
             dma((2, heads)),
@@ -405,8 +509,8 @@
             dma((n_wa - 1, heads, 4)),
             dma((n_wa - 1, heads, 4)),
             dma((heads, 4)),
-            dma((n_sa - 1, heads)),
-            dma((n_sa - 1, heads)),
+            dma((2, heads, n_sa)),
+            dma((2, heads, n_sa)),
             dma((n_wa - 1, heads)),
             dma((n_wa - 1, heads)),
         ],
@@ -414,9 +518,16 @@
             collective_id=0, has_side_effects=True, vmem_limit_bytes=60 * 1024 * 1024
         ),
     )(
-        window_ext, queries.reshape(flat), keys.reshape(flat), values.reshape(flat),
+        window_ext.T, queries.reshape(flat), keys.reshape(flat), values.reshape(flat),
         out_grad.reshape(flat), text_keys, text_values,
     )
+    text_sum = jax.ShapeDtypeStruct((text_rows, channels), F32)
+    outs = pl.pallas_call(
+        hand_over,
+        out_shape=(cell_out,) * 4 + (text_sum,) * 2,
+        in_specs=[in_vmem] * 6,
+        out_specs=(in_vmem,) * 6,
+    )(*outs)
     return tuple(out.reshape(grid) for out in outs[:4]) + tuple(outs[4:])
 
 

time: 91.2 us -> 77.2 us (0.85)
  local copies, waits for them, and re-layouts: 8.47 us -> 0 us
  Pallas kernels: 81.6 us -> 76.3 us
    unnamed x19 -> x0, local copies, waits for them, and re-layouts: 8.47 us -> none
    pallas_call x1, Pallas kernels: 81.6 us -> 73.4 us  [shards(): pl.pallas_call(functools.partial(kernel, n_sa, n_wa, heads, cells, text_r...]
    pallas_call x0 -> x1, Pallas kernels: none -> 2.88 us  [shards(): pl.pallas_call(hand_over, out_shape=(cell_out,) * 4 + (text_sum,) * 2, in...]
where the time goes in v2:
time: 77.2 us; the launch traced here: 77 us
  Pallas kernels  76.3 us (99%)
    pallas_call x1, Pallas kernels, shards(): pl.pallas_call(functools.partial(kernel, n_sa, n_wa, heads, cells, text_r...  73.4 us
    pallas_call x1, Pallas kernels, shards(): pl.pallas_call(hand_over, out_shape=(cell_out,) * 4 + (text_sum,) * 2, in...  2.88 us

profile of v2, /device:TPU:0, one launch (start us, length us, event | category | flops | bytes accessed | tf_op | source)
XLA Modules:
  0.0 77.0 jit_solution(4436620802209723381)
XLA Ops:
  0.6 73.4 %shard_map.118 = (bf16[128,1536]{1,0:T(8,128)(2,1)}, bf16[128,1536]{1,0:T(8,128)(2,1)}, bf16[128,1536]{1,0:T(8,128)(2,1)}, bf16[128,1536]{1,0:T(8,128)(2,1)}, bf...) custom-call(s32[3,12]{1,0:T(4,128)} %bitcast.13, bf16[128,1536]{1,0:T(8,128)(2,1)} %bitcast.9, ...), custom_call_target="tpu_custom_call" | custom-call | tf_op jit(solution)/shard_map/pallas_call | solution.py:480
  74.1 2.9 %shard_map.119 = (bf16[128,1536]{1,0:T(8,128)(2,1)}, bf16[128,1536]{1,0:T(8,128)(2,1)}, bf16[128,1536]{1,0:T(8,128)(2,1)}, bf16[128,1536]{1,0:T(8,128)(2,1)}, f32[64,1536]{1,0:T(8,128)}, /*index=5*/f32[64,1536]{1,0:T(8,128)}) custom-call(bf16[128,1536]{1,0:T(8,128)(2,1)} %get-tuple-element.18.refs_0_, bf16[128,1536]{1,0:T(8,128)(2,1)} %get-tuple-element.19.refs_1_, ...), custom_call_target="tpu_custom_call" | custom-call | tf_op jit(solution)/shard_map/pallas_call | solution.py:525
